TPU v7x, 256 devices: a whole 4x4x8 slice. The times are simulated.
256 devices in a mesh: scen: 16 (over y, x), lx: 4 (over z_lo, core), ly: 4 (over z_hi).
Axes of the slice: x: 4, y: 4, z: 8 (z_hi: 4, z_lo: 2; z = z_hi * 2 + z_lo), core: 2. Of those that a mesh axis runs over, the one named last changes fastest.
Arguments:
- density: float32 [16, 512, 2048], P('scen', 'lx', 'ly'), may hold values from 0.2 to 1.5
- trait: float32 [16, 512, 2048], P('scen', 'lx', 'ly'), may hold values from -4 to 4
- variance: float32 [16, 512, 2048], P('scen', 'lx', 'ly'), may hold values from 0.1 to 1
- optimum: float32 [16, 512, 2048], P('scen', 'lx', 'ly'), may hold values from -4 to 4
- observed: float32 [16, 512, 2048], P('scen', 'lx', 'ly'), may hold values from 0 to 1.5
- obs_step: int32 [16, 512], P('scen', 'lx'), may hold values from 1 to 2
- land_code: int32 [512, 2048], P('lx', 'ly'), may hold values 0 or 1
- maps: float32 [2, 512, 2048], P(None, 'lx', 'ly'), may hold values from -4 to 4
- first_moment: float32 [2, 512, 2048], P(None, 'lx', 'ly'), may hold values from -3 to 3
- second_moment: float32 [2, 512, 2048], P(None, 'lx', 'ly'), may hold values from 0.01 to 1
Outputs:
- new_maps: float32 [2, 512, 2048], P(None, 'lx', 'ly')
- new_first: float32 [2, 512, 2048], P(None, 'lx', 'ly')
- new_second: float32 [2, 512, 2048], P(None, 'lx', 'ly')
Inputs may be any that keep to these rules, and one draw needn't show every extreme that they name: `land_code`: 1 marks land, 0 sea.
All inputs are finite; a program needn't handle non-finite values. No bound on the sum of `land_code` on one device may be relied on, other than what follows from the above.
Results may differ from a plain program's by a relative error of at most 0.0003.
Values sent between devices are 32-bit elements; how exact they have to be, the bound alone decides.
A program may use at most 64 MiB of HBM per device.

v0:
```python
import jax
import jax.numpy as jnp
from jax import lax
from jax.sharding import PartitionSpec as P

STEPS = 2
ADAM_STEP = 10
REACH_MAX = 0.2
PRIOR_WEIGHT = 0.1
GROWTH_RATE = 0.5
MUTATION_INPUT = 0.02
LEARN_RATE = 0.01
BETA_FIRST = 0.9
BETA_SECOND = 0.999
ADAM_EPS = 1e-08
LOSS_WEIGHT = 2.0


def extended(block, sides, width):
    for axis, dim in sides:
        count = lax.axis_size(axis)
        forward = [(i, i + 1) for i in range(count - 1)]
        backward = [(target, source) for source, target in forward]
        low = lax.ppermute(
            lax.slice_in_dim(block, block.shape[dim] - width, None, axis=dim), axis, forward
        )
        high = lax.ppermute(lax.slice_in_dim(block, 0, width, axis=dim), axis, backward)
        block = jnp.concatenate([low, block, high], axis=dim)
    return block


def interior(values):
    return values[..., 1:-1, 1:-1]


def advance(fields, raw_maps, optimum_map, land_frac):
    density_now, trait_now, variance_now = (fields[0], fields[1], fields[2])
    reach_map = REACH_MAX * jax.nn.sigmoid(raw_maps[0])
    selection = jax.nn.softplus(interior(raw_maps[1]))
    carried = density_now * trait_now
    moment_two = density_now * (variance_now + trait_now * trait_now)
    reach_mid = interior(reach_map)
    land_mid = interior(land_frac)
    cuts = (
        (slice(2, None), slice(1, -1)),
        (slice(None, -2), slice(1, -1)),
        (slice(1, -1), slice(2, None)),
        (slice(1, -1), slice(None, -2)),
    )
    spread_density = interior(density_now)
    spread_carried = interior(carried)
    spread_moment = interior(moment_two)
    for row_cut, col_cut in cuts:
        weight = (
            0.5 * (reach_mid + reach_map[row_cut, col_cut]) * land_mid * land_frac[row_cut, col_cut]
        )
        spread_density = spread_density + weight * (
            density_now[row_cut, col_cut] - interior(density_now)
        )
        spread_carried = spread_carried + weight * (carried[row_cut, col_cut] - interior(carried))
        spread_moment = spread_moment + weight * (
            moment_two[row_cut, col_cut] - interior(moment_two)
        )
    trait_mid = interior(trait_now)
    variance_mid = interior(variance_now)
    denominator = spread_density + PRIOR_WEIGHT
    trait_spread = (spread_carried + PRIOR_WEIGHT * trait_mid) / denominator
    second_spread = (
        spread_moment + PRIOR_WEIGHT * (variance_mid + trait_mid * trait_mid)
    ) / denominator
    variance_spread = second_spread - trait_spread * trait_spread
    offset = trait_spread - interior(optimum_map)
    growth = land_mid * (
        GROWTH_RATE * (1.0 - spread_density) - 0.5 * selection * (offset * offset + variance_spread)
    )
    density_new = spread_density * jnp.exp(growth)
    response = selection * variance_spread
    trait_new = trait_spread - response * offset / (1.0 + response)
    variance_new = variance_spread / (1.0 + response) + MUTATION_INPUT
    return jnp.stack([density_new, trait_new, variance_new])


def adam_update(raw_maps, first_now, second_now, gradient):
    first_new = BETA_FIRST * first_now + (1.0 - BETA_FIRST) * gradient
    second_new = BETA_SECOND * second_now + (1.0 - BETA_SECOND) * gradient * gradient
    first_hat = first_new / (1.0 - BETA_FIRST**ADAM_STEP)
    second_hat = second_new / (1.0 - BETA_SECOND**ADAM_STEP)
    maps_new = raw_maps - LEARN_RATE * first_hat / (jnp.sqrt(second_hat) + ADAM_EPS)
    return (maps_new, first_new, second_new)


def state_halo(fields):
    return extended(fields, (("lx", 1), ("ly", 2)), 2)


def adjoint_halo(adjoint_now):
    return extended(adjoint_now, (("lx", 1), ("ly", 2)), 1)


def shards(
    density,
    trait,
    variance,
    optimum,
    observed,
    obs_step,
    land_code,
    maps,
    first_moment,
    second_moment,
):
    land_frac = land_code.astype(jnp.float32)
    statics = jnp.concatenate([maps, optimum, land_frac[None]], axis=0)
    fields = jnp.concatenate([density, trait, variance], axis=0)
    padded_states = []
    later_states = []
    static_wide = extended(statics, (("lx", 1), ("ly", 2)), 2)
    raw_near = interior(static_wide[0:2])
    optimum_near = interior(static_wide[2])
    land_near = interior(static_wide[3])
    for step_index in range(STEPS):
        padded = state_halo(fields)
        padded_states.append(padded)
        fields = advance(interior(padded), raw_near, optimum_near, land_near)
        later_states.append(fields)
    raw_wide = static_wide[0:2]
    optimum_wide = static_wide[2]
    land_wide = static_wide[3]
    chosen_rows = obs_step[0]

    def forward_wide(field_block, raw_block):
        return advance(field_block, raw_block, optimum_wide, land_wide)

    adjoint_now = jnp.zeros_like(later_states[-1])
    gradient = jnp.zeros(maps.shape, jnp.float32)
    for step_index in reversed(range(STEPS)):
        chosen = (chosen_rows == step_index + 1).astype(jnp.float32)[:, None]
        source = (
            2.0 * LOSS_WEIGHT * chosen * land_frac * (later_states[step_index][0] - observed[0])
        )
        blank = jnp.zeros_like(source)
        adjoint_now = adjoint_now + jnp.stack([source, blank, blank])
        adjoint_wide = adjoint_halo(adjoint_now)
        outputs, pullback = jax.vjp(forward_wide, padded_states[step_index], raw_wide)
        cot_fields, cot_maps = pullback(adjoint_wide)
        adjoint_now = cot_fields[:, 2:-2, 2:-2]
        gradient = gradient + cot_maps[:, 2:-2, 2:-2]
    share = lax.psum_scatter(gradient, "scen", scatter_dimension=1, tiled=True)
    share_rows = share.shape[1]
    row_start = lax.axis_index("scen") * share_rows
    maps_own = lax.dynamic_slice_in_dim(maps, row_start, share_rows, 1)
    first_own = lax.dynamic_slice_in_dim(first_moment, row_start, share_rows, 1)
    second_own = lax.dynamic_slice_in_dim(second_moment, row_start, share_rows, 1)
    maps_part, first_part, second_part = adam_update(maps_own, first_own, second_own, share)
    new_maps, new_first, new_second = (
        lax.all_gather(maps_part, "scen", axis=1, tiled=True),
        lax.all_gather(first_part, "scen", axis=1, tiled=True),
        lax.all_gather(second_part, "scen", axis=1, tiled=True),
    )
    return (new_maps, new_first, new_second)


def solution(mesh):
    in_specs = (
        P("scen", "lx", "ly"),
        P("scen", "lx", "ly"),
        P("scen", "lx", "ly"),
        P("scen", "lx", "ly"),
        P("scen", "lx", "ly"),
        P("scen", "lx"),
        P("lx", "ly"),
        P(None, "lx", "ly"),
        P(None, "lx", "ly"),
        P(None, "lx", "ly"),
    )
    out_specs = (P(None, "lx", "ly"), P(None, "lx", "ly"), P(None, "lx", "ly"))
    return jax.shard_map(shards, mesh=mesh, in_specs=in_specs, out_specs=out_specs, check_vma=False)
```

profile of v0, /device:TPU:32, one launch (start us, length us, event | category | flops | bytes accessed | tf_op | source)
XLA Modules:
  0.0 307.5 jit_solution(4712670643608340800)
XLA Ops:
  7.2 1.0 constant_dynamic-update-slice_fusion.2
  8.3 1.0 constant_dynamic-update-slice_fusion.1
  9.3 1.0 constant_dynamic-update-slice_fusion
  10.3 1.9 collective-permute-start
  12.2 3.6 %collective-permute-start.1 = (f32[3,2,512]{2,1,0:T(2,128)S(1)}, f32[3,2,512]{2,1,0:T(2,128)S(1)}, u32[]{:S(2)}, u32[]{:S(2)}) collective-permute-start(f32[3,2,512]{2,1,0:T(2,128)S(1)} %get-tuple-element.120), channel_id=1, source_target_pairs={{4,0},{8,4},{12,8},{5,1},{9,5},{13,9},{6,2},{10,6},{14,10},{7,3},{... | collective-permute-start | bytes 36872 | tf_op jit(solution)/shard_map/ppermute | solution.py:27
  15.9 1.9 collective-permute-start.4
  17.9 3.6 %collective-permute-start.5 = (f32[4,2,512]{2,1,0:T(2,128)S(1)}, f32[4,2,512]{2,1,0:T(2,128)S(1)}, u32[]{:S(2)}, u32[]{:S(2)}) collective-permute-start(f32[4,2,512]{2,1,0:T(2,128)S(1)} %get-tuple-element.86), channel_id=1, source_target_pairs={{4,0},{8,4},{12,8},{5,1},{9,5},{13,9},{6,2},{10,6},{14,10},{7,3},{... | collective-permute-start | bytes 49160 | tf_op jit(solution)/shard_map/ppermute | solution.py:27
  21.7 5.2 %collective-permute-start.2 = (f32[3,132,2]{2,1,0:T(8,128)S(1)}, f32[3,132,2]{2,1,0:T(8,128)S(1)}, u32[]{:S(2)}, u32[]{:S(2)}) collective-permute-start(f32[3,132,2]{2,1,0:T(8,128)S(1)} %get-tuple-element.109), channel_id=1, source_target_pairs={{0,1},{1,2},{2,3},{4,5},{5,6},{6,7},{8,9},{9,10},{10,11},{12,13},{... | collective-permute-start | bytes 9512 | tf_op jit(solution)/shard_map/ppermute | solution.py:24
  26.9 1.3 collective-permute-start.3
  28.2 6.2 %collective-permute-done.2 = f32[3,132,2]{2,1,0:T(8,128)S(1)} collective-permute-done((f32[3,132,2]{2,1,0:T(8,128)S(1)}, f32[3,132,2]{2,1,0:T(8,128)S(1)}, u32[]{:S(2)}, u32[]{:S(2)}) %collective-permute-start.2) | collective-permute-done | bytes 3200 | tf_op jit(solution)/shard_map/ppermute | solution.py:24
  34.4 3.0 collective-permute-done.3
  37.4 0.4 pad_maximum_fusion.1
  38.4 8.1 %collective-permute-start.6 = (f32[4,132,2]{2,1,0:T(8,128)S(1)}, f32[4,132,2]{2,1,0:T(8,128)S(1)}, u32[]{:S(2)}, u32[]{:S(2)}) collective-permute-start(f32[4,132,2]{2,1,0:T(8,128)S(1)} %get-tuple-element.83), channel_id=1, source_target_pairs={{0,1},{1,2},{2,3},{4,5},{5,6},{6,7},{8,9},{9,10},{10,11},{12,13},{... | collective-permute-start | bytes 12680 | tf_op jit(solution)/shard_map/ppermute | solution.py:24
  46.5 1.3 collective-permute-start.7
  48.1 7.9 %collective-permute-done.6 = f32[4,132,2]{2,1,0:T(8,128)S(1)} collective-permute-done((f32[4,132,2]{2,1,0:T(8,128)S(1)}, f32[4,132,2]{2,1,0:T(8,128)S(1)}, u32[]{:S(2)}, u32[]{:S(2)}) %collective-permute-start.6) | collective-permute-done | bytes 4256 | tf_op jit(solution)/shard_map/ppermute | solution.py:24
  56.0 5.7 %collective-permute-done.7 = f32[4,132,2]{2,1,0:T(8,128)S(1)} collective-permute-done((f32[4,132,2]{2,1,0:T(8,128)S(1)}, f32[4,132,2]{2,1,0:T(8,128)S(1)}, u32[]{:S(2)}, u32[]{:S(2)}) %collective-permute-start.7) | collective-permute-done | bytes 4256 | tf_op jit(solution)/shard_map/ppermute | solution.py:27
  61.7 0.6 pad_maximum_fusion
  62.7 1.0 fusion.93
  63.7 1.1 fusion.111
  65.1 1.9 collective-permute-start.8
  67.1 3.6 %collective-permute-start.9 = (f32[3,2,512]{2,1,0:T(2,128)S(1)}, f32[3,2,512]{2,1,0:T(2,128)S(1)}, u32[]{:S(2)}, u32[]{:S(2)}) collective-permute-start(f32[3,2,512]{2,1,0:T(2,128)S(1)} %get-tuple-element.118), channel_id=1, source_target_pairs={{4,0},{8,4},{12,8},{5,1},{9,5},{13,9},{6,2},{10,6},{14,10},{7,3},{... | collective-permute-start | bytes 36872 | tf_op jit(solution)/shard_map/ppermute | solution.py:27
  70.7 1.4 collective-permute-done.9
  72.2 3.1 collective-permute-start.10
  75.3 1.3 collective-permute-start.11
  76.7 5.9 %collective-permute-done.10 = f32[3,132,2]{2,1,0:T(8,128)S(1)} collective-permute-done((f32[3,132,2]{2,1,0:T(8,128)S(1)}, f32[3,132,2]{2,1,0:T(8,128)S(1)}, u32[]{:S(2)}, u32[]{:S(2)}) %collective-permute-start.10) | collective-permute-done | bytes 3200 | tf_op jit(solution)/shard_map/ppermute | solution.py:24
  82.6 5.3 %collective-permute-done.11 = f32[3,132,2]{2,1,0:T(8,128)S(1)} collective-permute-done((f32[3,132,2]{2,1,0:T(8,128)S(1)}, f32[3,132,2]{2,1,0:T(8,128)S(1)}, u32[]{:S(2)}, u32[]{:S(2)}) %collective-permute-start.11) | collective-permute-done | bytes 3200 | tf_op jit(solution)/shard_map/ppermute | solution.py:27
  87.9 0.4 pad_maximum_fusion.2
  88.3 0.4 slice_bitcast_fusion.15
  89.1 1.4 fusion.109
  90.5 1.9 collective-permute-start.12
  92.4 3.6 %collective-permute-start.13 = (f32[3,1,512]{2,1,0:T(1,128)S(1)}, f32[3,1,512]{2,1,0:T(1,128)S(1)}, u32[]{:S(2)}, u32[]{:S(2)}) collective-permute-start(f32[3,1,512]{2,1,0:T(1,128)S(1)} %get-tuple-element.148), channel_id=1, source_target_pairs={{4,0},{8,4},{12,8},{5,1},{9,5},{13,9},{6,2},{10,6},{14,10},{7,3},{... | collective-permute-start | bytes 18440 | tf_op jit(solution)/shard_map/ppermute | solution.py:27
  96.3 1.1 collective-permute-done.13
  97.5 3.2 %collective-permute-start.14 = (f32[3,130,1]{2,1,0:T(8,128)S(1)}, f32[3,130,1]{2,1,0:T(8,128)S(1)}, u32[]{:S(2)}, u32[]{:S(2)}) collective-permute-start(f32[3,130,1]{2,1,0:T(8,128)S(1)} %get-tuple-element.113), channel_id=1, source_target_pairs={{0,1},{1,2},{2,3},{4,5},{5,6},{6,7},{8,9},{9,10},{10,11},{12,13},{... | collective-permute-start | bytes 4688 | tf_op jit(solution)/shard_map/ppermute | solution.py:24
  100.7 1.5 collective-permute-start.15
  102.3 5.8 %collective-permute-done.14 = f32[3,130,1]{2,1,0:T(8,128)S(1)} collective-permute-done((f32[3,130,1]{2,1,0:T(8,128)S(1)}, f32[3,130,1]{2,1,0:T(8,128)S(1)}, u32[]{:S(2)}, u32[]{:S(2)}) %collective-permute-start.14) | collective-permute-done | bytes 1592 | tf_op jit(solution)/shard_map/ppermute | solution.py:24
  108.0 5.3 %collective-permute-done.15 = f32[3,130,1]{2,1,0:T(8,128)S(1)} collective-permute-done((f32[3,130,1]{2,1,0:T(8,128)S(1)}, f32[3,130,1]{2,1,0:T(8,128)S(1)}, u32[]{:S(2)}, u32[]{:S(2)}) %collective-permute-start.15) | collective-permute-done | bytes 1592 | tf_op jit(solution)/shard_map/ppermute | solution.py:27
  113.3 0.4 pad_maximum_fusion.3
  113.8 2.4 add_multiply_fusion.2
  116.2 2.3 add_add_fusion.7
  118.6 0.6 fusion.128
  119.2 1.1 add_bitcast_fusion.1
  120.3 1.1 fusion.3
  121.4 1.0 add_bitcast_fusion
  122.7 1.9 collective-permute-start.16
  124.7 3.6 %collective-permute-start.17 = (f32[3,1,512]{2,1,0:T(1,128)S(1)}, f32[3,1,512]{2,1,0:T(1,128)S(1)}, u32[]{:S(2)}, u32[]{:S(2)}) collective-permute-start(f32[3,1,512]{2,1,0:T(1,128)S(1)} %get-tuple-element.116), channel_id=1, source_target_pairs={{4,0},{8,4},{12,8},{5,1},{9,5},{13,9},{6,2},{10,6},{14,10},{7,3},{... | collective-permute-start | bytes 18440 | tf_op jit(solution)/shard_map/ppermute | solution.py:27
  128.4 1.2 collective-permute-done.17
  129.8 3.1 %collective-permute-start.18 = (f32[3,130,1]{2,1,0:T(8,128)S(1)}, f32[3,130,1]{2,1,0:T(8,128)S(1)}, u32[]{:S(2)}, u32[]{:S(2)}) collective-permute-start(f32[3,130,1]{2,1,0:T(8,128)S(1)} %get-tuple-element.111), channel_id=1, source_target_pairs={{0,1},{1,2},{2,3},{4,5},{5,6},{6,7},{8,9},{9,10},{10,11},{12,13},{... | collective-permute-start | bytes 4688 | tf_op jit(solution)/shard_map/ppermute | solution.py:24
  132.9 1.5 collective-permute-start.19
  134.6 5.7 %collective-permute-done.18 = f32[3,130,1]{2,1,0:T(8,128)S(1)} collective-permute-done((f32[3,130,1]{2,1,0:T(8,128)S(1)}, f32[3,130,1]{2,1,0:T(8,128)S(1)}, u32[]{:S(2)}, u32[]{:S(2)}) %collective-permute-start.18) | collective-permute-done | bytes 1592 | tf_op jit(solution)/shard_map/ppermute | solution.py:24
  140.2 5.3 %collective-permute-done.19 = f32[3,130,1]{2,1,0:T(8,128)S(1)} collective-permute-done((f32[3,130,1]{2,1,0:T(8,128)S(1)}, f32[3,130,1]{2,1,0:T(8,128)S(1)}, u32[]{:S(2)}, u32[]{:S(2)}) %collective-permute-start.19) | collective-permute-done | bytes 1592 | tf_op jit(solution)/shard_map/ppermute | solution.py:27
  145.6 0.4 pad_maximum_fusion.4
  146.0 2.0 add_multiply_fusion
  148.1 0.9 add_divide_fusion.1
  149.1 2.3 add_add_fusion.5
  151.4 0.9 multiply_bitcast_fusion.1
  152.2 1.2 fusion.1
  153.4 75.6 %reduce-scatter.2.cloned.1.call-done = f32[2,8,512]{2,1,0:T(8,128)} async-done(((f32[2,128,512]{2,1,0:T(8,128)}), f32[2,8,512]{2,1,0:T(8,128)}) %reduce-scatter.2.cloned.1.call-update) | async-done | bytes 32784 | tf_op jit(solution)/shard_map/reduce_scatter | solution.py:148
  229.1 0.8 divide_subtract_fusion
  229.9 23.3 %all_gather.9 = f32[2,128,512]{2,1,0:T(8,128)S(1)} all-gather(f32[2,8,512]{2,1,0:T(8,128)S(1)} %get-tuple-element.7), channel_id=1, replica_groups=mesh['scen'=16,'lx'=4,'ly'=4] {'scen'}, dimensions={1}, use_global_device_ids=true | all-gather | bytes 557056 | tf_op jit(solution)/shard_map/all_gather | solution.py:156
  253.2 22.1 %all_gather.10 = f32[2,128,512]{2,1,0:T(8,128)S(1)} all-gather(f32[2,8,512]{2,1,0:T(8,128)S(1)} %get-tuple-element.8), channel_id=1, replica_groups=mesh['scen'=16,'lx'=4,'ly'=4] {'scen'}, dimensions={1}, use_global_device_ids=true | all-gather | bytes 557056 | tf_op jit(solution)/shard_map/all_gather | solution.py:157
  275.3 23.0 %all_gather.11 = f32[2,128,512]{2,1,0:T(8,128)S(1)} all-gather(f32[2,8,512]{2,1,0:T(8,128)S(1)} %get-tuple-element.9), channel_id=1, replica_groups=mesh['scen'=16,'lx'=4,'ly'=4] {'scen'}, dimensions={1}, use_global_device_ids=true | all-gather | bytes 557056 | tf_op jit(solution)/shard_map/all_gather | solution.py:158
  298.3 0.8 copy.18
  299.1 0.8 copy.19
  299.9 0.8 copy.20
  (45 shorter events, 3.6 us)
Async XLA Ops:
  7.2 8.7 %copy-start.1 = (s32[128,512]{1,0:T(8,128)S(1)}, s32[128,512]{1,0:T(8,128)}, u32[]{:S(2)}) copy-start(s32[128,512]{1,0:T(8,128)} %param.17) | copy-start | bytes 786436
  7.2 8.7 %copy-start.2 = (f32[1,128,512]{2,1,0:T(8,128)S(1)}, f32[1,128,512]{2,1,0:T(8,128)}, u32[]{:S(2)}) copy-start(f32[1,128,512]{2,1,0:T(8,128)} %param.14) | copy-start | bytes 786436
  7.2 8.7 %copy-start = (f32[2,128,512]{2,1,0:T(8,128)S(1)}, f32[2,128,512]{2,1,0:T(8,128)}, u32[]{:S(2)}) copy-start(f32[2,128,512]{2,1,0:T(8,128)} %param.18) | copy-start | bytes 1572868
  7.2 221.9 %reduce-scatter.2.cloned.1.call-start = ((), (), s32[]{:S(2)}) async-start(), calls=%async_computation.1 | async-start | bytes 557056 | tf_op jit(solution)/shard_map/reduce_scatter | solution.py:148
  10.3 11.3 %collective-permute-start = (f32[3,2,512]{2,1,0:T(2,128)S(1)}, f32[3,2,512]{2,1,0:T(2,128)S(1)}, u32[]{:S(2)}, u32[]{:S(2)}) collective-permute-start(f32[3,2,512]{2,1,0:T(2,128)S(1)} %get-tuple-element.119), channel_id=1, source_target_pairs={{0,4},{4,8},{8,12},{1,5},{5,9},{9,13},{2,6},{6,10},{10,14},{3,7},{... | collective-permute-start | bytes 36872 | tf_op jit(solution)/shard_map/ppermute | solution.py:24
  12.2 16.0 %copy-start.4 = (s32[1,128]{1,0:T(1,128)S(1)}, s32[1,128]{1,0:T(1,128)}, u32[]{:S(2)}) copy-start(s32[1,128]{1,0:T(1,128)} %param.16) | copy-start | bytes 1540
  12.2 9.3 %collective-permute-start.1 = (f32[3,2,512]{2,1,0:T(2,128)S(1)}, f32[3,2,512]{2,1,0:T(2,128)S(1)}, u32[]{:S(2)}, u32[]{:S(2)}) collective-permute-start(f32[3,2,512]{2,1,0:T(2,128)S(1)} %get-tuple-element.120), channel_id=1, source_target_pairs={{4,0},{8,4},{12,8},{5,1},{9,5},{13,9},{6,2},{10,6},{14,10},{7,3},{... | collective-permute-start | bytes 36872 | tf_op jit(solution)/shard_map/ppermute | solution.py:27
  15.9 22.3 %collective-permute-start.4 = (f32[4,2,512]{2,1,0:T(2,128)S(1)}, f32[4,2,512]{2,1,0:T(2,128)S(1)}, u32[]{:S(2)}, u32[]{:S(2)}) collective-permute-start(f32[4,2,512]{2,1,0:T(2,128)S(1)} %get-tuple-element.85), channel_id=1, source_target_pairs={{0,4},{4,8},{8,12},{1,5},{5,9},{9,13},{2,6},{6,10},{10,14},{3,7},{... | collective-permute-start | bytes 49160 | tf_op jit(solution)/shard_map/ppermute | solution.py:24
  17.9 20.3 %collective-permute-start.5 = (f32[4,2,512]{2,1,0:T(2,128)S(1)}, f32[4,2,512]{2,1,0:T(2,128)S(1)}, u32[]{:S(2)}, u32[]{:S(2)}) collective-permute-start(f32[4,2,512]{2,1,0:T(2,128)S(1)} %get-tuple-element.86), channel_id=1, source_target_pairs={{4,0},{8,4},{12,8},{5,1},{9,5},{13,9},{6,2},{10,6},{14,10},{7,3},{... | collective-permute-start | bytes 49160 | tf_op jit(solution)/shard_map/ppermute | solution.py:27
  21.7 12.7 %collective-permute-start.2 = (f32[3,132,2]{2,1,0:T(8,128)S(1)}, f32[3,132,2]{2,1,0:T(8,128)S(1)}, u32[]{:S(2)}, u32[]{:S(2)}) collective-permute-start(f32[3,132,2]{2,1,0:T(8,128)S(1)} %get-tuple-element.109), channel_id=1, source_target_pairs={{0,1},{1,2},{2,3},{4,5},{5,6},{6,7},{8,9},{9,10},{10,11},{12,13},{... | collective-permute-start | bytes 9512 | tf_op jit(solution)/shard_map/ppermute | solution.py:24
  26.9 10.5 %collective-permute-start.3 = (f32[3,132,2]{2,1,0:T(8,128)S(1)}, f32[3,132,2]{2,1,0:T(8,128)S(1)}, u32[]{:S(2)}, u32[]{:S(2)}) collective-permute-start(f32[3,132,2]{2,1,0:T(8,128)S(1)} %get-tuple-element.110), channel_id=1, source_target_pairs={{1,0},{2,1},{3,2},{5,4},{6,5},{7,6},{9,8},{10,9},{11,10},{13,12},{... | collective-permute-start | bytes 9512 | tf_op jit(solution)/shard_map/ppermute | solution.py:27
  38.4 17.6 %collective-permute-start.6 = (f32[4,132,2]{2,1,0:T(8,128)S(1)}, f32[4,132,2]{2,1,0:T(8,128)S(1)}, u32[]{:S(2)}, u32[]{:S(2)}) collective-permute-start(f32[4,132,2]{2,1,0:T(8,128)S(1)} %get-tuple-element.83), channel_id=1, source_target_pairs={{0,1},{1,2},{2,3},{4,5},{5,6},{6,7},{8,9},{9,10},{10,11},{12,13},{... | collective-permute-start | bytes 12680 | tf_op jit(solution)/shard_map/ppermute | solution.py:24
  46.5 15.3 %collective-permute-start.7 = (f32[4,132,2]{2,1,0:T(8,128)S(1)}, f32[4,132,2]{2,1,0:T(8,128)S(1)}, u32[]{:S(2)}, u32[]{:S(2)}) collective-permute-start(f32[4,132,2]{2,1,0:T(8,128)S(1)} %get-tuple-element.84), channel_id=1, source_target_pairs={{1,0},{2,1},{3,2},{5,4},{6,5},{7,6},{9,8},{10,9},{11,10},{13,12},{... | collective-permute-start | bytes 12680 | tf_op jit(solution)/shard_map/ppermute | solution.py:27
  62.7 1.0 copy-start.3
  65.1 5.6 %collective-permute-start.8 = (f32[3,2,512]{2,1,0:T(2,128)S(1)}, f32[3,2,512]{2,1,0:T(2,128)S(1)}, u32[]{:S(2)}, u32[]{:S(2)}) collective-permute-start(f32[3,2,512]{2,1,0:T(2,128)S(1)} %get-tuple-element.117), channel_id=1, source_target_pairs={{0,4},{4,8},{8,12},{1,5},{5,9},{9,13},{2,6},{6,10},{10,14},{3,7},{... | collective-permute-start | bytes 36872 | tf_op jit(solution)/shard_map/ppermute | solution.py:24
  67.1 5.0 %collective-permute-start.9 = (f32[3,2,512]{2,1,0:T(2,128)S(1)}, f32[3,2,512]{2,1,0:T(2,128)S(1)}, u32[]{:S(2)}, u32[]{:S(2)}) collective-permute-start(f32[3,2,512]{2,1,0:T(2,128)S(1)} %get-tuple-element.118), channel_id=1, source_target_pairs={{4,0},{8,4},{12,8},{5,1},{9,5},{13,9},{6,2},{10,6},{14,10},{7,3},{... | collective-permute-start | bytes 36872 | tf_op jit(solution)/shard_map/ppermute | solution.py:27
  72.2 10.4 %collective-permute-start.10 = (f32[3,132,2]{2,1,0:T(8,128)S(1)}, f32[3,132,2]{2,1,0:T(8,128)S(1)}, u32[]{:S(2)}, u32[]{:S(2)}) collective-permute-start(f32[3,132,2]{2,1,0:T(8,128)S(1)} %get-tuple-element.107), channel_id=1, source_target_pairs={{0,1},{1,2},{2,3},{4,5},{5,6},{6,7},{8,9},{9,10},{10,11},{12,13},{... | collective-permute-start | bytes 9512 | tf_op jit(solution)/shard_map/ppermute | solution.py:24
  75.3 12.6 %collective-permute-start.11 = (f32[3,132,2]{2,1,0:T(8,128)S(1)}, f32[3,132,2]{2,1,0:T(8,128)S(1)}, u32[]{:S(2)}, u32[]{:S(2)}) collective-permute-start(f32[3,132,2]{2,1,0:T(8,128)S(1)} %get-tuple-element.108), channel_id=1, source_target_pairs={{1,0},{2,1},{3,2},{5,4},{6,5},{7,6},{9,8},{10,9},{11,10},{13,12},{... | collective-permute-start | bytes 9512 | tf_op jit(solution)/shard_map/ppermute | solution.py:27
  90.5 5.8 %collective-permute-start.12 = (f32[3,1,512]{2,1,0:T(1,128)S(1)}, f32[3,1,512]{2,1,0:T(1,128)S(1)}, u32[]{:S(2)}, u32[]{:S(2)}) collective-permute-start(f32[3,1,512]{2,1,0:T(1,128)S(1)} %get-tuple-element.147), channel_id=1, source_target_pairs={{0,4},{4,8},{8,12},{1,5},{5,9},{9,13},{2,6},{6,10},{10,14},{3,7},{... | collective-permute-start | bytes 18440 | tf_op jit(solution)/shard_map/ppermute | solution.py:24
  92.4 5.0 %collective-permute-start.13 = (f32[3,1,512]{2,1,0:T(1,128)S(1)}, f32[3,1,512]{2,1,0:T(1,128)S(1)}, u32[]{:S(2)}, u32[]{:S(2)}) collective-permute-start(f32[3,1,512]{2,1,0:T(1,128)S(1)} %get-tuple-element.148), channel_id=1, source_target_pairs={{4,0},{8,4},{12,8},{5,1},{9,5},{13,9},{6,2},{10,6},{14,10},{7,3},{... | collective-permute-start | bytes 18440 | tf_op jit(solution)/shard_map/ppermute | solution.py:27
  97.5 10.5 %collective-permute-start.14 = (f32[3,130,1]{2,1,0:T(8,128)S(1)}, f32[3,130,1]{2,1,0:T(8,128)S(1)}, u32[]{:S(2)}, u32[]{:S(2)}) collective-permute-start(f32[3,130,1]{2,1,0:T(8,128)S(1)} %get-tuple-element.113), channel_id=1, source_target_pairs={{0,1},{1,2},{2,3},{4,5},{5,6},{6,7},{8,9},{9,10},{10,11},{12,13},{... | collective-permute-start | bytes 4688 | tf_op jit(solution)/shard_map/ppermute | solution.py:24
  100.7 12.7 %collective-permute-start.15 = (f32[3,130,1]{2,1,0:T(8,128)S(1)}, f32[3,130,1]{2,1,0:T(8,128)S(1)}, u32[]{:S(2)}, u32[]{:S(2)}) collective-permute-start(f32[3,130,1]{2,1,0:T(8,128)S(1)} %get-tuple-element.114), channel_id=1, source_target_pairs={{1,0},{2,1},{3,2},{5,4},{6,5},{7,6},{9,8},{10,9},{11,10},{13,12},{... | collective-permute-start | bytes 4688 | tf_op jit(solution)/shard_map/ppermute | solution.py:27
  122.7 5.7 %collective-permute-start.16 = (f32[3,1,512]{2,1,0:T(1,128)S(1)}, f32[3,1,512]{2,1,0:T(1,128)S(1)}, u32[]{:S(2)}, u32[]{:S(2)}) collective-permute-start(f32[3,1,512]{2,1,0:T(1,128)S(1)} %get-tuple-element.115), channel_id=1, source_target_pairs={{0,4},{4,8},{8,12},{1,5},{5,9},{9,13},{2,6},{6,10},{10,14},{3,7},{... | collective-permute-start | bytes 18440 | tf_op jit(solution)/shard_map/ppermute | solution.py:24
  124.7 5.0 %collective-permute-start.17 = (f32[3,1,512]{2,1,0:T(1,128)S(1)}, f32[3,1,512]{2,1,0:T(1,128)S(1)}, u32[]{:S(2)}, u32[]{:S(2)}) collective-permute-start(f32[3,1,512]{2,1,0:T(1,128)S(1)} %get-tuple-element.116), channel_id=1, source_target_pairs={{4,0},{8,4},{12,8},{5,1},{9,5},{13,9},{6,2},{10,6},{14,10},{7,3},{... | collective-permute-start | bytes 18440 | tf_op jit(solution)/shard_map/ppermute | solution.py:27
  129.8 10.5 %collective-permute-start.18 = (f32[3,130,1]{2,1,0:T(8,128)S(1)}, f32[3,130,1]{2,1,0:T(8,128)S(1)}, u32[]{:S(2)}, u32[]{:S(2)}) collective-permute-start(f32[3,130,1]{2,1,0:T(8,128)S(1)} %get-tuple-element.111), channel_id=1, source_target_pairs={{0,1},{1,2},{2,3},{4,5},{5,6},{6,7},{8,9},{9,10},{10,11},{12,13},{... | collective-permute-start | bytes 4688 | tf_op jit(solution)/shard_map/ppermute | solution.py:24
  132.9 12.7 %collective-permute-start.19 = (f32[3,130,1]{2,1,0:T(8,128)S(1)}, f32[3,130,1]{2,1,0:T(8,128)S(1)}, u32[]{:S(2)}, u32[]{:S(2)}) collective-permute-start(f32[3,130,1]{2,1,0:T(8,128)S(1)} %get-tuple-element.112), channel_id=1, source_target_pairs={{1,0},{2,1},{3,2},{5,4},{6,5},{7,6},{9,8},{10,9},{11,10},{13,12},{... | collective-permute-start | bytes 4688 | tf_op jit(solution)/shard_map/ppermute | solution.py:27
Sparse Core Ops, SparseCore 0:
  153.5 75.4 reduce-scatter.1
where the time goes:
time: 308 us
  waiting for transfers between devices  135 us (44%)
  blocking collectives  68.4 us (22%)
  starting transfers between devices  57.4 us (19%)
  other arithmetic  25 us (8%)
  between operations  14.6 us (5%)
  local copies, waits for them, and re-layouts  6.75 us (2%)
    reduce_scatter x1, waiting for transfers between devices, shards(): share = lax.psum_scatter(gradient, 'scen', scatter_dimension=1, tiled=True)  75.6 us
    ppermute x10, starting transfers between devices, extended(): lax.ppermute(lax.slice_in_dim(block, block.shape[dim] - width, None, axis...  32.2 us
    ppermute x10, waiting for transfers between devices, extended(): lax.ppermute(lax.slice_in_dim(block, block.shape[dim] - width, None, axis...  31.4 us
    ppermute x10, waiting for transfers between devices, extended(): lax.ppermute(lax.slice_in_dim(block, 0, width, axis=dim), axis, backward)  28.4 us
    ppermute x10, starting transfers between devices, extended(): lax.ppermute(lax.slice_in_dim(block, 0, width, axis=dim), axis, backward)  25.1 us
    all_gather x1, blocking collectives, shards(): lax.all_gather(maps_part, 'scen', axis=1, tiled=True)  23.3 us
    all_gather x1, blocking collectives, shards(): lax.all_gather(second_part, 'scen', axis=1, tiled=True)  23 us
    all_gather x1, blocking collectives, shards(): lax.all_gather(first_part, 'scen', axis=1, tiled=True)  22.1 us
  transfers between devices with their start and end apart: 21, of which 14 were waited for; matrix products, arithmetic and copies ran while one was open for 1% of the time, Pallas kernels for 0%

commit v1 on v0

--- a/solution.py
+++ b/solution.py
@@ -14,6 +14,13 @@
 BETA_SECOND = 0.999
 ADAM_EPS = 1e-08
 LOSS_WEIGHT = 2.0
+
+
+def swapped_in(x, mesh_axis, d):
+    size = lax.axis_size(mesh_axis)
+    tiles = jnp.stack([x for _ in range(size)])
+    tiles = lax.all_to_all(tiles, mesh_axis, split_axis=0, concat_axis=0)
+    return jnp.concatenate(tiles, axis=d)
 
 
 def extended(block, sides, width):
@@ -153,7 +160,7 @@
     second_own = lax.dynamic_slice_in_dim(second_moment, row_start, share_rows, 1)
     maps_part, first_part, second_part = adam_update(maps_own, first_own, second_own, share)
     new_maps, new_first, new_second = (
-        lax.all_gather(maps_part, "scen", axis=1, tiled=True),
+        swapped_in(maps_part, "scen", 1),
         lax.all_gather(first_part, "scen", axis=1, tiled=True),
         lax.all_gather(second_part, "scen", axis=1, tiled=True),
     )

time: 308 us -> 294 us (0.955)
  blocking collectives: 68.4 us -> 48 us
  starting transfers between devices: 57.4 us -> 62.3 us
    all_gather x1 -> x0, blocking collectives: 23.3 us -> none  [shards(): lax.all_gather(maps_part, 'scen', axis=1, tiled=True)]
    all_to_all x0 -> x1, starting transfers between devices: none -> 4.99 us  [swapped_in(): tiles = lax.all_to_all(tiles, mesh_axis, split_axis=0, concat_axis=0)]
  transfers between devices with their start and end apart: 21 -> 22, of which waited for: 14 -> 14; matrix products, arithmetic and copies ran while one was open for 1% -> 1% of each run, Pallas kernels for 0% -> 0%
where the time goes in v1:
time: 294 us; the launch traced here: 293 us
  waiting for transfers between devices  135 us (46%)
  starting transfers between devices  62.3 us (21%)
  blocking collectives  48 us (16%)
  other arithmetic  25 us (9%)
  between operations  14.6 us (5%)
  local copies, waits for them, and re-layouts  7.64 us (3%)
    reduce_scatter x1, waiting for transfers between devices, shards(): share = lax.psum_scatter(gradient, 'scen', scatter_dimension=1, tiled=True)  75.6 us
    ppermute x10, starting transfers between devices, extended(): lax.ppermute(lax.slice_in_dim(block, block.shape[dim] - width, None, axis...  32.2 us
    ppermute x10, waiting for transfers between devices, extended(): lax.ppermute(lax.slice_in_dim(block, block.shape[dim] - width, None, axis...  31.4 us
    ppermute x10, waiting for transfers between devices, extended(): lax.ppermute(lax.slice_in_dim(block, 0, width, axis=dim), axis, backward)  28.4 us
    all_gather x1, blocking collectives, shards(): lax.all_gather(first_part, 'scen', axis=1, tiled=True)  25.2 us
    ppermute x10, starting transfers between devices, extended(): lax.ppermute(lax.slice_in_dim(block, 0, width, axis=dim), axis, backward)  25.1 us
    all_gather x1, blocking collectives, shards(): lax.all_gather(second_part, 'scen', axis=1, tiled=True)  22.9 us
  transfers between devices with their start and end apart: 22, of which 14 were waited for; matrix products, arithmetic and copies ran while one was open for 1% of the time, Pallas kernels for 0%

profile of v1, /device:TPU:32, one launch (start us, length us, event | category | flops | bytes accessed | tf_op | source)
XLA Modules:
  0.0 293.0 jit_solution(4613335232087056575)
XLA Ops:
  7.2 1.0 constant_dynamic-update-slice_fusion.2
  8.3 1.0 constant_dynamic-update-slice_fusion.1
  9.3 1.0 constant_dynamic-update-slice_fusion
  10.3 1.9 collective-permute-start
  12.2 3.6 %collective-permute-start.1 = (f32[3,2,512]{2,1,0:T(2,128)S(1)}, f32[3,2,512]{2,1,0:T(2,128)S(1)}, u32[]{:S(2)}, u32[]{:S(2)}) collective-permute-start(f32[3,2,512]{2,1,0:T(2,128)S(1)} %get-tuple-element.120), channel_id=1, source_target_pairs={{4,0},{8,4},{12,8},{5,1},{9,5},{13,9},{6,2},{10,6},{14,10},{7,3},{... | collective-permute-start | bytes 36872 | tf_op jit(solution)/shard_map/ppermute | solution.py:34
  15.9 1.9 collective-permute-start.4
  17.9 3.6 %collective-permute-start.5 = (f32[4,2,512]{2,1,0:T(2,128)S(1)}, f32[4,2,512]{2,1,0:T(2,128)S(1)}, u32[]{:S(2)}, u32[]{:S(2)}) collective-permute-start(f32[4,2,512]{2,1,0:T(2,128)S(1)} %get-tuple-element.86), channel_id=1, source_target_pairs={{4,0},{8,4},{12,8},{5,1},{9,5},{13,9},{6,2},{10,6},{14,10},{7,3},{... | collective-permute-start | bytes 49160 | tf_op jit(solution)/shard_map/ppermute | solution.py:34
  21.7 5.2 %collective-permute-start.2 = (f32[3,132,2]{2,1,0:T(8,128)S(1)}, f32[3,132,2]{2,1,0:T(8,128)S(1)}, u32[]{:S(2)}, u32[]{:S(2)}) collective-permute-start(f32[3,132,2]{2,1,0:T(8,128)S(1)} %get-tuple-element.109), channel_id=1, source_target_pairs={{0,1},{1,2},{2,3},{4,5},{5,6},{6,7},{8,9},{9,10},{10,11},{12,13},{... | collective-permute-start | bytes 9512 | tf_op jit(solution)/shard_map/ppermute | solution.py:31
  26.9 1.3 collective-permute-start.3
  28.2 6.2 %collective-permute-done.2 = f32[3,132,2]{2,1,0:T(8,128)S(1)} collective-permute-done((f32[3,132,2]{2,1,0:T(8,128)S(1)}, f32[3,132,2]{2,1,0:T(8,128)S(1)}, u32[]{:S(2)}, u32[]{:S(2)}) %collective-permute-start.2) | collective-permute-done | bytes 3200 | tf_op jit(solution)/shard_map/ppermute | solution.py:31
  34.4 3.0 %collective-permute-done.3 = f32[3,132,2]{2,1,0:T(8,128)S(1)} collective-permute-done((f32[3,132,2]{2,1,0:T(8,128)S(1)}, f32[3,132,2]{2,1,0:T(8,128)S(1)}, u32[]{:S(2)}, u32[]{:S(2)}) %collective-permute-start.3) | collective-permute-done | bytes 3200 | tf_op jit(solution)/shard_map/ppermute | solution.py:34
  37.4 0.4 pad_maximum_fusion.1
  38.4 8.1 %collective-permute-start.6 = (f32[4,132,2]{2,1,0:T(8,128)S(1)}, f32[4,132,2]{2,1,0:T(8,128)S(1)}, u32[]{:S(2)}, u32[]{:S(2)}) collective-permute-start(f32[4,132,2]{2,1,0:T(8,128)S(1)} %get-tuple-element.83), channel_id=1, source_target_pairs={{0,1},{1,2},{2,3},{4,5},{5,6},{6,7},{8,9},{9,10},{10,11},{12,13},{... | collective-permute-start | bytes 12680 | tf_op jit(solution)/shard_map/ppermute | solution.py:31
  46.5 1.3 collective-permute-start.7
  48.1 7.9 %collective-permute-done.6 = f32[4,132,2]{2,1,0:T(8,128)S(1)} collective-permute-done((f32[4,132,2]{2,1,0:T(8,128)S(1)}, f32[4,132,2]{2,1,0:T(8,128)S(1)}, u32[]{:S(2)}, u32[]{:S(2)}) %collective-permute-start.6) | collective-permute-done | bytes 4256 | tf_op jit(solution)/shard_map/ppermute | solution.py:31
  56.0 5.7 %collective-permute-done.7 = f32[4,132,2]{2,1,0:T(8,128)S(1)} collective-permute-done((f32[4,132,2]{2,1,0:T(8,128)S(1)}, f32[4,132,2]{2,1,0:T(8,128)S(1)}, u32[]{:S(2)}, u32[]{:S(2)}) %collective-permute-start.7) | collective-permute-done | bytes 4256 | tf_op jit(solution)/shard_map/ppermute | solution.py:34
  61.7 0.6 pad_maximum_fusion
  62.7 1.0 fusion.93
  63.7 1.1 fusion.111
  65.1 1.9 collective-permute-start.8
  67.1 3.6 %collective-permute-start.9 = (f32[3,2,512]{2,1,0:T(2,128)S(1)}, f32[3,2,512]{2,1,0:T(2,128)S(1)}, u32[]{:S(2)}, u32[]{:S(2)}) collective-permute-start(f32[3,2,512]{2,1,0:T(2,128)S(1)} %get-tuple-element.118), channel_id=1, source_target_pairs={{4,0},{8,4},{12,8},{5,1},{9,5},{13,9},{6,2},{10,6},{14,10},{7,3},{... | collective-permute-start | bytes 36872 | tf_op jit(solution)/shard_map/ppermute | solution.py:34
  70.7 1.4 collective-permute-done.9
  72.3 3.1 %collective-permute-start.10 = (f32[3,132,2]{2,1,0:T(8,128)S(1)}, f32[3,132,2]{2,1,0:T(8,128)S(1)}, u32[]{:S(2)}, u32[]{:S(2)}) collective-permute-start(f32[3,132,2]{2,1,0:T(8,128)S(1)} %get-tuple-element.107), channel_id=1, source_target_pairs={{0,1},{1,2},{2,3},{4,5},{5,6},{6,7},{8,9},{9,10},{10,11},{12,13},{... | collective-permute-start | bytes 9512 | tf_op jit(solution)/shard_map/ppermute | solution.py:31
  75.3 1.3 collective-permute-start.11
  76.7 5.9 %collective-permute-done.10 = f32[3,132,2]{2,1,0:T(8,128)S(1)} collective-permute-done((f32[3,132,2]{2,1,0:T(8,128)S(1)}, f32[3,132,2]{2,1,0:T(8,128)S(1)}, u32[]{:S(2)}, u32[]{:S(2)}) %collective-permute-start.10) | collective-permute-done | bytes 3200 | tf_op jit(solution)/shard_map/ppermute | solution.py:31
  82.6 5.3 %collective-permute-done.11 = f32[3,132,2]{2,1,0:T(8,128)S(1)} collective-permute-done((f32[3,132,2]{2,1,0:T(8,128)S(1)}, f32[3,132,2]{2,1,0:T(8,128)S(1)}, u32[]{:S(2)}, u32[]{:S(2)}) %collective-permute-start.11) | collective-permute-done | bytes 3200 | tf_op jit(solution)/shard_map/ppermute | solution.py:34
  87.9 0.4 pad_maximum_fusion.2
  89.1 1.4 fusion.109
  90.5 1.9 collective-permute-start.12
  92.4 3.6 %collective-permute-start.13 = (f32[3,1,512]{2,1,0:T(1,128)S(1)}, f32[3,1,512]{2,1,0:T(1,128)S(1)}, u32[]{:S(2)}, u32[]{:S(2)}) collective-permute-start(f32[3,1,512]{2,1,0:T(1,128)S(1)} %get-tuple-element.148), channel_id=1, source_target_pairs={{4,0},{8,4},{12,8},{5,1},{9,5},{13,9},{6,2},{10,6},{14,10},{7,3},{... | collective-permute-start | bytes 18440 | tf_op jit(solution)/shard_map/ppermute | solution.py:34
  96.3 1.1 collective-permute-done.13
  97.5 3.2 %collective-permute-start.14 = (f32[3,130,1]{2,1,0:T(8,128)S(1)}, f32[3,130,1]{2,1,0:T(8,128)S(1)}, u32[]{:S(2)}, u32[]{:S(2)}) collective-permute-start(f32[3,130,1]{2,1,0:T(8,128)S(1)} %get-tuple-element.113), channel_id=1, source_target_pairs={{0,1},{1,2},{2,3},{4,5},{5,6},{6,7},{8,9},{9,10},{10,11},{12,13},{... | collective-permute-start | bytes 4688 | tf_op jit(solution)/shard_map/ppermute | solution.py:31
  100.7 1.5 collective-permute-start.15
  102.3 5.8 %collective-permute-done.14 = f32[3,130,1]{2,1,0:T(8,128)S(1)} collective-permute-done((f32[3,130,1]{2,1,0:T(8,128)S(1)}, f32[3,130,1]{2,1,0:T(8,128)S(1)}, u32[]{:S(2)}, u32[]{:S(2)}) %collective-permute-start.14) | collective-permute-done | bytes 1592 | tf_op jit(solution)/shard_map/ppermute | solution.py:31
  108.1 5.3 %collective-permute-done.15 = f32[3,130,1]{2,1,0:T(8,128)S(1)} collective-permute-done((f32[3,130,1]{2,1,0:T(8,128)S(1)}, f32[3,130,1]{2,1,0:T(8,128)S(1)}, u32[]{:S(2)}, u32[]{:S(2)}) %collective-permute-start.15) | collective-permute-done | bytes 1592 | tf_op jit(solution)/shard_map/ppermute | solution.py:34
  113.4 0.4 pad_maximum_fusion.3
  113.8 2.4 add_multiply_fusion.2
  116.2 2.4 add_add_fusion.7
  118.6 0.6 fusion.128
  119.3 1.1 add_bitcast_fusion.1
  120.3 1.1 fusion.3
  121.4 1.0 add_bitcast_fusion
  122.7 1.9 collective-permute-start.16
  124.7 3.6 %collective-permute-start.17 = (f32[3,1,512]{2,1,0:T(1,128)S(1)}, f32[3,1,512]{2,1,0:T(1,128)S(1)}, u32[]{:S(2)}, u32[]{:S(2)}) collective-permute-start(f32[3,1,512]{2,1,0:T(1,128)S(1)} %get-tuple-element.116), channel_id=1, source_target_pairs={{4,0},{8,4},{12,8},{5,1},{9,5},{13,9},{6,2},{10,6},{14,10},{7,3},{... | collective-permute-start | bytes 18440 | tf_op jit(solution)/shard_map/ppermute | solution.py:34
  128.4 1.2 collective-permute-done.17
  129.8 3.1 %collective-permute-start.18 = (f32[3,130,1]{2,1,0:T(8,128)S(1)}, f32[3,130,1]{2,1,0:T(8,128)S(1)}, u32[]{:S(2)}, u32[]{:S(2)}) collective-permute-start(f32[3,130,1]{2,1,0:T(8,128)S(1)} %get-tuple-element.111), channel_id=1, source_target_pairs={{0,1},{1,2},{2,3},{4,5},{5,6},{6,7},{8,9},{9,10},{10,11},{12,13},{... | collective-permute-start | bytes 4688 | tf_op jit(solution)/shard_map/ppermute | solution.py:31
  132.9 1.5 collective-permute-start.19
  134.6 5.7 %collective-permute-done.18 = f32[3,130,1]{2,1,0:T(8,128)S(1)} collective-permute-done((f32[3,130,1]{2,1,0:T(8,128)S(1)}, f32[3,130,1]{2,1,0:T(8,128)S(1)}, u32[]{:S(2)}, u32[]{:S(2)}) %collective-permute-start.18) | collective-permute-done | bytes 1592 | tf_op jit(solution)/shard_map/ppermute | solution.py:31
  140.3 5.3 %collective-permute-done.19 = f32[3,130,1]{2,1,0:T(8,128)S(1)} collective-permute-done((f32[3,130,1]{2,1,0:T(8,128)S(1)}, f32[3,130,1]{2,1,0:T(8,128)S(1)}, u32[]{:S(2)}, u32[]{:S(2)}) %collective-permute-start.19) | collective-permute-done | bytes 1592 | tf_op jit(solution)/shard_map/ppermute | solution.py:34
  145.6 0.4 pad_maximum_fusion.4
  146.0 2.0 add_multiply_fusion
  148.1 0.9 add_divide_fusion.1
  149.1 2.3 add_add_fusion.5
  151.3 0.9 multiply_bitcast_fusion.1
  152.2 1.2 fusion.1
  153.4 75.6 %reduce-scatter.2.cloned.1.call-done = f32[2,8,512]{2,1,0:T(8,128)} async-done(((f32[2,128,512]{2,1,0:T(8,128)}), f32[2,8,512]{2,1,0:T(8,128)}) %reduce-scatter.2.cloned.1.call-update) | async-done | bytes 32784 | tf_op jit(solution)/shard_map/reduce_scatter | solution.py:155
  229.0 0.8 divide_subtract_fusion
  229.9 0.9 stack.51
  230.7 5.0 %all-to-all-start = ((f32[16,2,8,512]{3,2,1,0:T(8,128)}), f32[16,2,8,512]{3,2,1,0:T(8,128)S(1)}, u32[]{:S(2)}, u32[]{:S(2)}) async-start(f32[16,2,8,512]{3,2,1,0:T(8,128)} %stack.51), calls=%async_computation.1 | async-start | bytes 1048576 | tf_op jit(solution)/shard_map/all_to_all | solution.py:22
  235.7 25.2 %all_gather.6 = f32[2,128,512]{2,1,0:T(8,128)S(1)} all-gather(f32[2,8,512]{2,1,0:T(8,128)S(1)} %get-tuple-element.8), channel_id=1, replica_groups=mesh['scen'=16,'lx'=4,'ly'=4] {'scen'}, dimensions={1}, use_global_device_ids=true | all-gather | bytes 557056 | tf_op jit(solution)/shard_map/all_gather | solution.py:164
  260.9 22.9 %all_gather.7 = f32[2,128,512]{2,1,0:T(8,128)S(1)} all-gather(f32[2,8,512]{2,1,0:T(8,128)S(1)} %get-tuple-element.9), channel_id=1, replica_groups=mesh['scen'=16,'lx'=4,'ly'=4] {'scen'}, dimensions={1}, use_global_device_ids=true | all-gather | bytes 557056 | tf_op jit(solution)/shard_map/all_gather | solution.py:165
  283.7 0.8 copy.15
  284.6 0.8 copy.20
  285.4 0.8 copy.21
  (47 shorter events, 4.0 us)
Async XLA Ops:
  7.2 8.7 %copy-start.1 = (s32[128,512]{1,0:T(8,128)S(1)}, s32[128,512]{1,0:T(8,128)}, u32[]{:S(2)}) copy-start(s32[128,512]{1,0:T(8,128)} %param.17) | copy-start | bytes 786436
  7.2 8.7 %copy-start.2 = (f32[1,128,512]{2,1,0:T(8,128)S(1)}, f32[1,128,512]{2,1,0:T(8,128)}, u32[]{:S(2)}) copy-start(f32[1,128,512]{2,1,0:T(8,128)} %param.14) | copy-start | bytes 786436
  7.2 8.7 %copy-start = (f32[2,128,512]{2,1,0:T(8,128)S(1)}, f32[2,128,512]{2,1,0:T(8,128)}, u32[]{:S(2)}) copy-start(f32[2,128,512]{2,1,0:T(8,128)} %param.18) | copy-start | bytes 1572868
  7.2 221.8 %reduce-scatter.2.cloned.1.call-start = ((), (), s32[]{:S(2)}) async-start(), calls=%async_computation.2 | async-start | bytes 557056 | tf_op jit(solution)/shard_map/reduce_scatter | solution.py:155
  10.3 11.3 %collective-permute-start = (f32[3,2,512]{2,1,0:T(2,128)S(1)}, f32[3,2,512]{2,1,0:T(2,128)S(1)}, u32[]{:S(2)}, u32[]{:S(2)}) collective-permute-start(f32[3,2,512]{2,1,0:T(2,128)S(1)} %get-tuple-element.119), channel_id=1, source_target_pairs={{0,4},{4,8},{8,12},{1,5},{5,9},{9,13},{2,6},{6,10},{10,14},{3,7},{... | collective-permute-start | bytes 36872 | tf_op jit(solution)/shard_map/ppermute | solution.py:31
  12.2 16.0 %copy-start.4 = (s32[1,128]{1,0:T(1,128)S(1)}, s32[1,128]{1,0:T(1,128)}, u32[]{:S(2)}) copy-start(s32[1,128]{1,0:T(1,128)} %param.16) | copy-start | bytes 1540
  12.2 9.3 %collective-permute-start.1 = (f32[3,2,512]{2,1,0:T(2,128)S(1)}, f32[3,2,512]{2,1,0:T(2,128)S(1)}, u32[]{:S(2)}, u32[]{:S(2)}) collective-permute-start(f32[3,2,512]{2,1,0:T(2,128)S(1)} %get-tuple-element.120), channel_id=1, source_target_pairs={{4,0},{8,4},{12,8},{5,1},{9,5},{13,9},{6,2},{10,6},{14,10},{7,3},{... | collective-permute-start | bytes 36872 | tf_op jit(solution)/shard_map/ppermute | solution.py:34
  15.9 22.3 %collective-permute-start.4 = (f32[4,2,512]{2,1,0:T(2,128)S(1)}, f32[4,2,512]{2,1,0:T(2,128)S(1)}, u32[]{:S(2)}, u32[]{:S(2)}) collective-permute-start(f32[4,2,512]{2,1,0:T(2,128)S(1)} %get-tuple-element.85), channel_id=1, source_target_pairs={{0,4},{4,8},{8,12},{1,5},{5,9},{9,13},{2,6},{6,10},{10,14},{3,7},{... | collective-permute-start | bytes 49160 | tf_op jit(solution)/shard_map/ppermute | solution.py:31
  17.9 20.3 %collective-permute-start.5 = (f32[4,2,512]{2,1,0:T(2,128)S(1)}, f32[4,2,512]{2,1,0:T(2,128)S(1)}, u32[]{:S(2)}, u32[]{:S(2)}) collective-permute-start(f32[4,2,512]{2,1,0:T(2,128)S(1)} %get-tuple-element.86), channel_id=1, source_target_pairs={{4,0},{8,4},{12,8},{5,1},{9,5},{13,9},{6,2},{10,6},{14,10},{7,3},{... | collective-permute-start | bytes 49160 | tf_op jit(solution)/shard_map/ppermute | solution.py:34
  21.7 12.7 %collective-permute-start.2 = (f32[3,132,2]{2,1,0:T(8,128)S(1)}, f32[3,132,2]{2,1,0:T(8,128)S(1)}, u32[]{:S(2)}, u32[]{:S(2)}) collective-permute-start(f32[3,132,2]{2,1,0:T(8,128)S(1)} %get-tuple-element.109), channel_id=1, source_target_pairs={{0,1},{1,2},{2,3},{4,5},{5,6},{6,7},{8,9},{9,10},{10,11},{12,13},{... | collective-permute-start | bytes 9512 | tf_op jit(solution)/shard_map/ppermute | solution.py:31
  26.9 10.5 %collective-permute-start.3 = (f32[3,132,2]{2,1,0:T(8,128)S(1)}, f32[3,132,2]{2,1,0:T(8,128)S(1)}, u32[]{:S(2)}, u32[]{:S(2)}) collective-permute-start(f32[3,132,2]{2,1,0:T(8,128)S(1)} %get-tuple-element.110), channel_id=1, source_target_pairs={{1,0},{2,1},{3,2},{5,4},{6,5},{7,6},{9,8},{10,9},{11,10},{13,12},{... | collective-permute-start | bytes 9512 | tf_op jit(solution)/shard_map/ppermute | solution.py:34
  38.4 17.6 %collective-permute-start.6 = (f32[4,132,2]{2,1,0:T(8,128)S(1)}, f32[4,132,2]{2,1,0:T(8,128)S(1)}, u32[]{:S(2)}, u32[]{:S(2)}) collective-permute-start(f32[4,132,2]{2,1,0:T(8,128)S(1)} %get-tuple-element.83), channel_id=1, source_target_pairs={{0,1},{1,2},{2,3},{4,5},{5,6},{6,7},{8,9},{9,10},{10,11},{12,13},{... | collective-permute-start | bytes 12680 | tf_op jit(solution)/shard_map/ppermute | solution.py:31
  46.5 15.3 %collective-permute-start.7 = (f32[4,132,2]{2,1,0:T(8,128)S(1)}, f32[4,132,2]{2,1,0:T(8,128)S(1)}, u32[]{:S(2)}, u32[]{:S(2)}) collective-permute-start(f32[4,132,2]{2,1,0:T(8,128)S(1)} %get-tuple-element.84), channel_id=1, source_target_pairs={{1,0},{2,1},{3,2},{5,4},{6,5},{7,6},{9,8},{10,9},{11,10},{13,12},{... | collective-permute-start | bytes 12680 | tf_op jit(solution)/shard_map/ppermute | solution.py:34
  62.7 1.0 copy-start.3
  65.1 5.6 %collective-permute-start.8 = (f32[3,2,512]{2,1,0:T(2,128)S(1)}, f32[3,2,512]{2,1,0:T(2,128)S(1)}, u32[]{:S(2)}, u32[]{:S(2)}) collective-permute-start(f32[3,2,512]{2,1,0:T(2,128)S(1)} %get-tuple-element.117), channel_id=1, source_target_pairs={{0,4},{4,8},{8,12},{1,5},{5,9},{9,13},{2,6},{6,10},{10,14},{3,7},{... | collective-permute-start | bytes 36872 | tf_op jit(solution)/shard_map/ppermute | solution.py:31
  67.1 5.0 %collective-permute-start.9 = (f32[3,2,512]{2,1,0:T(2,128)S(1)}, f32[3,2,512]{2,1,0:T(2,128)S(1)}, u32[]{:S(2)}, u32[]{:S(2)}) collective-permute-start(f32[3,2,512]{2,1,0:T(2,128)S(1)} %get-tuple-element.118), channel_id=1, source_target_pairs={{4,0},{8,4},{12,8},{5,1},{9,5},{13,9},{6,2},{10,6},{14,10},{7,3},{... | collective-permute-start | bytes 36872 | tf_op jit(solution)/shard_map/ppermute | solution.py:34
  72.3 10.4 %collective-permute-start.10 = (f32[3,132,2]{2,1,0:T(8,128)S(1)}, f32[3,132,2]{2,1,0:T(8,128)S(1)}, u32[]{:S(2)}, u32[]{:S(2)}) collective-permute-start(f32[3,132,2]{2,1,0:T(8,128)S(1)} %get-tuple-element.107), channel_id=1, source_target_pairs={{0,1},{1,2},{2,3},{4,5},{5,6},{6,7},{8,9},{9,10},{10,11},{12,13},{... | collective-permute-start | bytes 9512 | tf_op jit(solution)/shard_map/ppermute | solution.py:31
  75.3 12.6 %collective-permute-start.11 = (f32[3,132,2]{2,1,0:T(8,128)S(1)}, f32[3,132,2]{2,1,0:T(8,128)S(1)}, u32[]{:S(2)}, u32[]{:S(2)}) collective-permute-start(f32[3,132,2]{2,1,0:T(8,128)S(1)} %get-tuple-element.108), channel_id=1, source_target_pairs={{1,0},{2,1},{3,2},{5,4},{6,5},{7,6},{9,8},{10,9},{11,10},{13,12},{... | collective-permute-start | bytes 9512 | tf_op jit(solution)/shard_map/ppermute | solution.py:34
  90.5 5.8 %collective-permute-start.12 = (f32[3,1,512]{2,1,0:T(1,128)S(1)}, f32[3,1,512]{2,1,0:T(1,128)S(1)}, u32[]{:S(2)}, u32[]{:S(2)}) collective-permute-start(f32[3,1,512]{2,1,0:T(1,128)S(1)} %get-tuple-element.147), channel_id=1, source_target_pairs={{0,4},{4,8},{8,12},{1,5},{5,9},{9,13},{2,6},{6,10},{10,14},{3,7},{... | collective-permute-start | bytes 18440 | tf_op jit(solution)/shard_map/ppermute | solution.py:31
  92.4 5.0 %collective-permute-start.13 = (f32[3,1,512]{2,1,0:T(1,128)S(1)}, f32[3,1,512]{2,1,0:T(1,128)S(1)}, u32[]{:S(2)}, u32[]{:S(2)}) collective-permute-start(f32[3,1,512]{2,1,0:T(1,128)S(1)} %get-tuple-element.148), channel_id=1, source_target_pairs={{4,0},{8,4},{12,8},{5,1},{9,5},{13,9},{6,2},{10,6},{14,10},{7,3},{... | collective-permute-start | bytes 18440 | tf_op jit(solution)/shard_map/ppermute | solution.py:34
  97.5 10.5 %collective-permute-start.14 = (f32[3,130,1]{2,1,0:T(8,128)S(1)}, f32[3,130,1]{2,1,0:T(8,128)S(1)}, u32[]{:S(2)}, u32[]{:S(2)}) collective-permute-start(f32[3,130,1]{2,1,0:T(8,128)S(1)} %get-tuple-element.113), channel_id=1, source_target_pairs={{0,1},{1,2},{2,3},{4,5},{5,6},{6,7},{8,9},{9,10},{10,11},{12,13},{... | collective-permute-start | bytes 4688 | tf_op jit(solution)/shard_map/ppermute | solution.py:31
  100.7 12.7 %collective-permute-start.15 = (f32[3,130,1]{2,1,0:T(8,128)S(1)}, f32[3,130,1]{2,1,0:T(8,128)S(1)}, u32[]{:S(2)}, u32[]{:S(2)}) collective-permute-start(f32[3,130,1]{2,1,0:T(8,128)S(1)} %get-tuple-element.114), channel_id=1, source_target_pairs={{1,0},{2,1},{3,2},{5,4},{6,5},{7,6},{9,8},{10,9},{11,10},{13,12},{... | collective-permute-start | bytes 4688 | tf_op jit(solution)/shard_map/ppermute | solution.py:34
  122.7 5.7 %collective-permute-start.16 = (f32[3,1,512]{2,1,0:T(1,128)S(1)}, f32[3,1,512]{2,1,0:T(1,128)S(1)}, u32[]{:S(2)}, u32[]{:S(2)}) collective-permute-start(f32[3,1,512]{2,1,0:T(1,128)S(1)} %get-tuple-element.115), channel_id=1, source_target_pairs={{0,4},{4,8},{8,12},{1,5},{5,9},{9,13},{2,6},{6,10},{10,14},{3,7},{... | collective-permute-start | bytes 18440 | tf_op jit(solution)/shard_map/ppermute | solution.py:31
  124.7 5.0 %collective-permute-start.17 = (f32[3,1,512]{2,1,0:T(1,128)S(1)}, f32[3,1,512]{2,1,0:T(1,128)S(1)}, u32[]{:S(2)}, u32[]{:S(2)}) collective-permute-start(f32[3,1,512]{2,1,0:T(1,128)S(1)} %get-tuple-element.116), channel_id=1, source_target_pairs={{4,0},{8,4},{12,8},{5,1},{9,5},{13,9},{6,2},{10,6},{14,10},{7,3},{... | collective-permute-start | bytes 18440 | tf_op jit(solution)/shard_map/ppermute | solution.py:34
  129.8 10.5 %collective-permute-start.18 = (f32[3,130,1]{2,1,0:T(8,128)S(1)}, f32[3,130,1]{2,1,0:T(8,128)S(1)}, u32[]{:S(2)}, u32[]{:S(2)}) collective-permute-start(f32[3,130,1]{2,1,0:T(8,128)S(1)} %get-tuple-element.111), channel_id=1, source_target_pairs={{0,1},{1,2},{2,3},{4,5},{5,6},{6,7},{8,9},{9,10},{10,11},{12,13},{... | collective-permute-start | bytes 4688 | tf_op jit(solution)/shard_map/ppermute | solution.py:31
  132.9 12.7 %collective-permute-start.19 = (f32[3,130,1]{2,1,0:T(8,128)S(1)}, f32[3,130,1]{2,1,0:T(8,128)S(1)}, u32[]{:S(2)}, u32[]{:S(2)}) collective-permute-start(f32[3,130,1]{2,1,0:T(8,128)S(1)} %get-tuple-element.112), channel_id=1, source_target_pairs={{1,0},{2,1},{3,2},{5,4},{6,5},{7,6},{9,8},{10,9},{11,10},{13,12},{... | collective-permute-start | bytes 4688 | tf_op jit(solution)/shard_map/ppermute | solution.py:34
  230.7 53.0 %all-to-all-start = ((f32[16,2,8,512]{3,2,1,0:T(8,128)}), f32[16,2,8,512]{3,2,1,0:T(8,128)S(1)}, u32[]{:S(2)}, u32[]{:S(2)}) async-start(f32[16,2,8,512]{3,2,1,0:T(8,128)} %stack.51), calls=%async_computation.1 | async-start | bytes 1048576 | tf_op jit(solution)/shard_map/all_to_all | solution.py:22
Sparse Core Ops, SparseCore 0:
  153.5 75.4 reduce-scatter.1
